TPU v7x, 32 devices: a whole 2x2x4 slice. The times are simulated.
32 devices in a mesh: row: 4 (over y, x), col: 8 (over z, core).
Axes of the slice: x: 2, y: 2, z: 4, core: 2. Of those that a mesh axis runs over, the one named last changes fastest.
Arguments:
- queries: bfloat16 [8, 512, 1024], P('col', 'row'), may hold values from -120 to 120
- keys: bfloat16 [8, 512, 128], P('col', 'row'), may hold values from -8 to 8
- values: bfloat16 [8, 512, 128], P('col', 'row'), may hold values from -6 to 6
- outputs: bfloat16 [8, 512, 1024], P('col', 'row'), may hold values from -6 to 6
- out_grad: bfloat16 [8, 512, 1024], P('col', 'row'), may hold values from -192 to 192
- positions: int32 [8, 512], P('col'), may hold values from 0 to 511, each once within a row
- tile_flags: int32 [8, 4, 4], P('col', 'row'), may hold values 0 or 1
Outputs:
- query_grad: bfloat16 [8, 512, 1024], P('col', 'row')
- key_grad: bfloat16 [8, 512, 128], P('col', 'row')
- value_grad: bfloat16 [8, 512, 128], P('col', 'row')
All inputs are finite; a program needn't handle non-finite values. No bound on the sum of `tile_flags` on one device may be relied on, other than what follows from the above.
Results may differ from a plain program's by a relative error of at most 0.0065.
Values may be sent and summed in bfloat16 or wider, within the bound.
No kernel may reach another device: no remote copies, remote signals or barrier semaphores. Data moves between devices by JAX's collectives and lax.ppermute only.
A program may use at most 64 MiB of HBM per device.

v0:
```python
import math

import jax
import jax.numpy as jnp
from jax import lax
from jax.sharding import PartitionSpec as P

H = 8
HD = 128


def combine_stats(left_pair, right_pair):
    larger = jnp.maximum(left_pair[0], right_pair[0])
    total = left_pair[1] * jnp.exp(left_pair[0] - larger) + right_pair[1] * jnp.exp(
        right_pair[0] - larger
    )
    return (larger, total)


def body(queries, keys, values, outputs, out_grad, positions, tile_flags):
    score_scale = 1.0 / math.sqrt(HD)
    row_at = lax.axis_index("row")
    key_all, value_all = (
        lax.all_gather(keys, "row", axis=1, tiled=True),
        lax.all_gather(values, "row", axis=1, tiled=True),
    )
    key_rows = key_all[0]
    value_rows = value_all[0]
    tokens = queries.shape[1]
    length = key_rows.shape[0]
    shards = length // tokens
    query_heads = queries[0].reshape(tokens, H, HD)
    grad_heads = out_grad[0].reshape(tokens, H, HD)
    output_heads = outputs[0].reshape(tokens, H, HD)
    trace_pos = positions[0]
    flag_row = tile_flags[0, 0]
    query_index = row_at * tokens + jnp.arange(tokens, dtype=jnp.int32)
    query_pos = lax.dynamic_slice_in_dim(trace_pos, row_at * tokens, tokens)
    blocks = length // tokens

    def block_allowed(start):
        key_index = start + jnp.arange(tokens, dtype=jnp.int32)
        key_pos = lax.dynamic_slice_in_dim(trace_pos, start, tokens)
        owner = key_index // tokens
        match = owner[:, None] == jnp.arange(shards, dtype=jnp.int32)[None, :]
        key_flag = jnp.sum(jnp.where(match, flag_row[None, :], 0), axis=1)
        return (key_pos[None, :] <= query_pos[:, None]) & (
            (key_flag[None, :] == 1) | (key_index[None, :] == query_index[:, None])
        )

    def block_scores(start):
        key_piece = lax.dynamic_slice_in_dim(key_rows, start, tokens, 0)
        return (
            jnp.einsum("qhd,kd->hqk", query_heads, key_piece, preferred_element_type=jnp.float32)
            * score_scale
        )

    def stats_step(step, carry):
        start = (step * tokens).astype(jnp.int32)
        allowed = block_allowed(start)
        masked = jnp.where(allowed[None], block_scores(start), -1e30)
        local_max = jnp.max(masked, axis=2)
        local_sum = jnp.sum(
            jnp.where(allowed[None], jnp.exp(masked - local_max[:, :, None]), 0.0), axis=2
        )
        return combine_stats(carry, (local_max, local_sum))

    start_stats = (jnp.full((H, tokens), -1e30, jnp.float32), jnp.zeros((H, tokens), jnp.float32))
    row_max, row_sum = lax.fori_loop(0, blocks, stats_step, start_stats)
    log_total = row_max + jnp.log(row_sum)
    out_dot = jnp.sum(grad_heads.astype(jnp.float32) * output_heads.astype(jnp.float32), axis=2).T

    def grad_step(step, buffers):
        start = (step * tokens).astype(jnp.int32)
        allowed = block_allowed(start)
        grad_buffer, weight_buffer = buffers
        weights = jnp.where(
            allowed[None], jnp.exp(block_scores(start) - log_total[:, :, None]), 0.0
        )
        value_piece = lax.dynamic_slice_in_dim(value_rows, start, tokens, 0)
        grad_probs = jnp.einsum(
            "qhd,kd->hqk", grad_heads, value_piece, preferred_element_type=jnp.float32
        )
        grad_scores = (weights * (grad_probs - out_dot[:, :, None]) * score_scale).astype(
            jnp.bfloat16
        )
        weights_low = weights.astype(jnp.bfloat16)
        grad_buffer = lax.dynamic_update_slice_in_dim(grad_buffer, grad_scores, start, 2)
        weight_buffer = lax.dynamic_update_slice_in_dim(weight_buffer, weights_low, start, 2)
        return (grad_buffer, weight_buffer)

    empty = jnp.zeros((H, tokens, length), jnp.bfloat16)
    grad_scores, weights_low = lax.fori_loop(0, blocks, grad_step, (empty, empty))
    query_grad = jnp.einsum(
        "hqk,kd->qhd", grad_scores, key_rows, preferred_element_type=jnp.float32
    )
    query_grad = query_grad.reshape(1, tokens, H * HD).astype(jnp.bfloat16)
    key_part = jnp.einsum(
        "hqk,qhd->kd", grad_scores, query_heads, preferred_element_type=jnp.float32
    )
    value_part = jnp.einsum(
        "hqk,qhd->kd", weights_low, grad_heads, preferred_element_type=jnp.float32
    )
    joined = lax.psum_scatter(
        jnp.concatenate([key_part, value_part], axis=1), "row", scatter_dimension=0, tiled=True
    )
    key_grad = joined[:, :HD]
    value_grad = joined[:, HD:]
    return (query_grad, key_grad[None].astype(jnp.bfloat16), value_grad[None].astype(jnp.bfloat16))


def solution(mesh):
    placed = (
        P("col", "row", None),
        P("col", "row", None),
        P("col", "row", None),
        P("col", "row", None),
        P("col", "row", None),
        P("col", None),
        P("col", "row", None),
    )
    return jax.shard_map(
        body,
        mesh=mesh,
        in_specs=placed,
        out_specs=(P("col", "row", None), P("col", "row", None), P("col", "row", None)),
        check_vma=False,
    )
```

profile of v0, /device:TPU:0, one launch (start us, length us, event | category | flops | bytes accessed | tf_op | source)
XLA Modules:
  0.0 76.7 jit_solution(11052119164415023996)
XLA Ops:
  7.2 0.9 %copy.36 = bf16[1,128,128]{1,2,0:T(8,128)(2,1)S(1)} copy(bf16[1,128,128]{2,1,0:T(8,128)(2,1)} %param.12) | data formatting | bytes 65536 | tf_op args[1]
  8.1 10.1 %all_gather.6 = bf16[1,512,128]{1,2,0:T(8,128)(2,1)S(1)} all-gather(bf16[1,128,128]{1,2,0:T(8,128)(2,1)S(1)} %copy.36), channel_id=1, replica_groups=mesh['row'=4,'col'=8] {'row'}, dimensions={1}, use_global_device_ids=true | all-gather | bytes 163840 | tf_op jit(solution)/shard_map/all_gather | solution.py:24
  18.3 0.6 copy-done.3
  18.9 8.4 %all_gather.7 = bf16[1,512,128]{2,1,0:T(8,128)(2,1)S(1)} all-gather(bf16[1,128,128]{2,1,0:T(8,128)(2,1)S(1)} %copy-done.3), channel_id=1, replica_groups=mesh['row'=4,'col'=8] {'row'}, dimensions={1}, use_global_device_ids=true | all-gather | bytes 163840 | tf_op jit(solution)/shard_map/all_gather | solution.py:25
  27.4 0.2 copy.37
  27.6 0.2 copy.43
  27.8 0.7 copy-done.4
  28.4 0.7 copy-done.5
  29.1 2.8 %while.37 = (s32[]{:T(128)}, f32[8,128]{1,0:T(8,128)S(1)}, f32[8,128]{1,0:T(8,128)S(1)}, s32[512]{0:T(512)S(1)}, s32[128]{0:T(128)S(1)}, /*index=5*/s32[1,1,4]{2...) while((s32[]{:T(128)}, f32[8,128]{1,0:T(8,128)S(1)}, ...), condition=%wide.region_4.5_spmd.clone, body=%wide.region_0.4_spmd.clone.sunk | while | flops 34416260 | bytes 1436125 | solution.py:69
  29.3 0.1 or_and_fusion.5
  29.4 0.2 fusion.48
  30.0 0.1 or_and_fusion.5
  30.1 0.2 fusion.48
  30.7 0.1 or_and_fusion.5
  30.8 0.2 fusion.48
  31.4 0.1 or_and_fusion.5
  31.5 0.2 fusion.48
  32.0 0.2 copy.41
  32.1 0.8 copy-done.2
  32.9 0.2 copy.40
  33.1 0.2 copy.44
  33.4 0.1 broadcast_in_dim.214.clone
  33.5 0.1 broadcast_in_dim.214
  33.7 6.5 %while.36 = (s32[]{:T(128)}, bf16[8,128,512]{1,2,0:T(8,128)(2,1)S(1)}, bf16[8,128,512]{1,2,0:T(8,128)(2,1)S(1)}, s32[512]{0:T(512)S(1)}, s32[128]{0:T(128)S(1)},...) while((s32[]{:T(128)}, ...), condition=%wide.region_8.9_spmd.clone, body=%wide.region_6.8_spmd.clone.sunk | while | flops 68226688 | bytes 2212419 | solution.py:93
  33.8 0.6 copy-done.6
  34.5 0.1 or_and_fusion.4
  34.6 0.3 convert_dynamic-update-slice_fusion.2
  35.0 0.3 fusion.46
  35.4 0.6 copy-done.6
  36.2 0.1 or_and_fusion.4
  36.3 0.3 convert_dynamic-update-slice_fusion.2
  36.6 0.3 fusion.46
  37.1 0.6 copy-done.6
  37.8 0.1 or_and_fusion.4
  37.9 0.3 convert_dynamic-update-slice_fusion.2
  38.3 0.3 fusion.46
  38.7 0.6 copy-done.6
  39.6 0.3 convert_dynamic-update-slice_fusion.2
  39.9 0.3 fusion.46
  40.2 0.5 convolution_bitcast_fusion.1
  40.7 0.5 convolution_bitcast_fusion.2
  41.2 0.8 %pad_maximum_fusion = f32[512,256]{0,1:T(8,128)} fusion(f32[512,128]{0,1:T(8,128)S(1)} %convolution_bitcast_fusion.1, f32[512,128]{0,1:T(8,128)S(1)} %convolution_bitcast_fusion.2), kind=kLoop, calls=%fused_computation.53 | loop fusion | flops 131072 | bytes 1048576 | tf_op jit(solution)/shard_map/concatenate | solution.py:105
  42.0 0.3 convolution_convert_fusion
  42.3 0.8 %copy.48 = bf16[1,128,1024]{2,1,0:T(8,128)(2,1)} copy(bf16[1,128,1024]{1,2,0:T(8,128)(2,1)S(1)} %bitcast.96) | data formatting | bytes 524288
  43.2 24.3 %reduce-scatter.2.cloned.1.call-done = f32[128,256]{0,1:T(8,128)} async-done(((f32[512,256]{0,1:T(8,128)}), f32[128,256]{0,1:T(8,128)}) %reduce-scatter.2.cloned.1.call-update) | async-done | bytes 131088 | tf_op jit(solution)/shard_map/reduce_scatter | solution.py:104
  67.5 0.9 %convert.5 = bf16[128,256]{0,1:T(8,128)(2,1)S(1)} convert(f32[128,256]{0,1:T(8,128)} %reduce-scatter.2.cloned.1.call-done) | non-fusion elementwise | flops 32768 | bytes 196608 | tf_op jit(solution)/shard_map/convert.2
  68.4 0.7 copy.50
  69.2 0.7 copy.49
  (70 shorter events, 2.4 us)
Async XLA Ops:
  7.2 60.4 %reduce-scatter.2.cloned.1.call-start = ((), (), s32[]{:S(2)}) async-start(), calls=%async_computation.1 | async-start | bytes 655360 | tf_op jit(solution)/shard_map/reduce_scatter | solution.py:104
  8.1 19.3 %copy-start = (bf16[1,128,1024]{2,1,0:T(8,128)(2,1)S(1)}, bf16[1,128,1024]{2,1,0:T(8,128)(2,1)}, u32[]{:S(2)}) copy-start(bf16[1,128,1024]{2,1,0:T(8,128)(2,1)} %param.11) | copy-start | bytes 786436
  18.2 0.8 copy-start.3
  27.7 0.7 copy-start.4
  28.4 0.7 copy-start.5
  29.1 2.9 %copy-start.1 = (bf16[1,128,1024]{2,1,0:T(8,128)(2,1)S(1)}, bf16[1,128,1024]{2,1,0:T(8,128)(2,1)}, u32[]{:S(2)}) copy-start(bf16[1,128,1024]{2,1,0:T(8,128)(2,1)} %param.14) | copy-start | bytes 786436
  31.9 1.0 %copy-start.2 = (bf16[1,128,1024]{2,1,0:T(8,128)(2,1)S(1)}, bf16[1,128,1024]{2,1,0:T(8,128)(2,1)}, u32[]{:S(2)}) copy-start(bf16[1,128,1024]{2,1,0:T(8,128)(2,1)} %param.15) | copy-start | bytes 786436
  33.8 0.7 copy-start.6
  35.4 0.7 copy-start.6
  37.0 0.7 copy-start.6
  38.7 0.7 copy-start.6
Sparse Core Ops, SparseCore 0:
  42.1 25.3 reduce-scatter.1
where the time goes:
time: 77.1 us; the launch traced here: 76.7 us
  waiting for transfers between devices  24.4 us (32%)
  blocking collectives  18.5 us (24%)
  between operations  14.2 us (18%)
  local copies, waits for them, and re-layouts  10.4 us (13%)
  matrix products  4.77 us (6%)
  other arithmetic  4.11 us (5%)
    reduce_scatter x1, waiting for transfers between devices, body(): lax.psum_scatter(jnp.concatenate([key_part, value_part], axis=1), 'row',...  24.3 us
    all_gather x1, blocking collectives, body(): lax.all_gather(keys, 'row', axis=1, tiled=True)  10.1 us
    all_gather x1, blocking collectives, body(): lax.all_gather(values, 'row', axis=1, tiled=True)  8.42 us
    unnamed x22, local copies, waits for them, and re-layouts  6.9 us
    while x8, local copies, waits for them, and re-layouts  2.6 us
    dot_general x8, matrix products, block_scores(): jnp.einsum('qhd,kd->hqk', query_heads, key_piece, preferred_element_type=...  2.35 us
  transfers between devices with their start and end apart: 1, of which 1 were waited for; matrix products, arithmetic and copies ran while one was open for 2% of the time, Pallas kernels for 0%

commit v1 on v0

v1 whole, which is shorter than its diff:
```python
import functools
import math

import jax
import jax.numpy as jnp
from jax import lax
from jax.experimental import pallas as pl
from jax.experimental.pallas import tpu as pltpu
from jax.sharding import PartitionSpec as P

HD = 128
SCALE = 1.0 / math.sqrt(HD)
EXP2_SCALE = SCALE * math.log2(math.e)
MASKED = -1e30
F32 = jnp.float32
BF16 = jnp.bfloat16
VMEM = pl.BlockSpec(memory_space=pltpu.VMEM)
HBM = pl.BlockSpec(memory_space=pltpu.HBM)
SMEM = pl.BlockSpec(memory_space=pltpu.SMEM)
GRANT = pltpu.CompilerParams(vmem_limit_bytes=16 << 20)


def peer_of(rank, step, n):
    if n & (n - 1) == 0:
        return rank ^ step
    return lax.rem(rank + step, n) if isinstance(rank, jax.Array) else (rank + step) % n


def dot_nt(a, b):
    return lax.dot_general(a, b, (((1,), (1,)), ((), ())), preferred_element_type=F32)


def dot_nn(a, b):
    return lax.dot_general(a, b, (((1,), (0,)), ((), ())), preferred_element_type=F32)


def pack_kernel(k_ref, v_ref, kv_ref, sems):
    copies = [
        pltpu.make_async_copy(k_ref.at[0], kv_ref.at[:, :HD], sems.at[0]),
        pltpu.make_async_copy(v_ref.at[0], kv_ref.at[:, HD:], sems.at[1]),
    ]
    for copy in copies:
        copy.start()
    for copy in copies:
        copy.wait()


def pre_kernel(
    n, heads, rank_ref, flag_ref, pos_ref, q_hbm, g_hbm, o_hbm, kv_ref,
    bias_ref, dot_ref, top_ref, sum_ref, exp_ref, diff_ref, q_ref, g_ref, o_ref, sems,
):
    tokens = q_ref.shape[1]
    copies = [
        pltpu.make_async_copy(src, dst, sems.at[i])
        for i, (src, dst) in enumerate([(q_hbm, q_ref), (g_hbm, g_ref), (o_hbm, o_ref)])
    ]
    for copy in copies:
        copy.start()
    rank = rank_ref[0]
    pos = pos_ref[...].astype(F32)
    here = pos_ref[pl.ds(rank, 1), :].astype(F32)
    for step in range(n):
        peer = peer_of(rank, step, n)
        key_pos = jnp.broadcast_to(pos_ref[pl.ds(peer, 1), :].astype(F32), (8, tokens)).T[:, :1]
        seen = jnp.where(flag_ref[0, 0, peer] == 1, here, -1.0)
        allowed = key_pos <= seen
        if step == 0:
            rows = lax.broadcasted_iota(jnp.int32, (tokens, tokens), 0)
            cols = lax.broadcasted_iota(jnp.int32, (tokens, tokens), 1)
            allowed = allowed | (rows == cols)
        bias_ref[step] = jnp.where(allowed, 0.0, MASKED).astype(F32)
    key = kv_ref[:, :HD]
    value = kv_ref[:, HD:]
    for copy in copies:
        copy.wait()
    for h in range(heads):
        at = pl.ds(h * HD, HD)
        g = g_ref[0, :, at]
        out_dot = jnp.sum((g.astype(F32) * o_ref[0, :, at].astype(F32)).T, axis=0, keepdims=True)
        dot_ref[h : h + 1, :] = out_dot
        t = dot_nt(key, q_ref[0, :, at]) * EXP2_SCALE + bias_ref[0]
        top = jnp.max(t, axis=0, keepdims=True)
        e = jnp.exp2(t - top)
        top_ref[h : h + 1, :] = top
        sum_ref[h : h + 1, :] = jnp.sum(e, axis=0, keepdims=True)
        exp_ref[:, at] = e
        diff_ref[:, at] = (dot_nt(value, g) - out_dot) * SCALE


def main_kernel(
    n, heads, q_ref, g_ref, bias_ref, dot_ref, top_ref, sum_ref, *refs,
):
    kv_refs, refs = refs[: n - 1], refs[n - 1 :]
    part_refs, (fac_ref, ds_ref, p_ref) = refs[: n - 1], refs[n - 1 :]
    tokens = q_ref.shape[1]
    key = jnp.concatenate([r[:, :HD] for r in kv_refs], axis=0)
    value = jnp.concatenate([r[:, HD:] for r in kv_refs], axis=0)
    bias = bias_ref[1:].reshape((n - 1) * tokens, tokens)
    for h in range(heads):
        at = pl.ds(h * HD, HD)
        own_top = top_ref[h : h + 1, :]
        t = dot_nt(key, q_ref[0, :, at]) * EXP2_SCALE + bias
        top = jnp.maximum(own_top, jnp.max(t, axis=0, keepdims=True))
        e = jnp.exp2(t - top)
        own = jnp.exp2(own_top - top)
        inv = 1.0 / (own * sum_ref[h : h + 1, :] + jnp.sum(e, axis=0, keepdims=True))
        fac_ref[h : h + 1, :] = own * inv
        p = e * inv
        p_ref[:, at] = p.astype(BF16)
        diff = dot_nt(value, g_ref[0, :, at]) - dot_ref[h : h + 1, :]
        ds_ref[:, at] = (p * (diff * SCALE)).astype(BF16)
    key_sum, value_sum = 0.0, 0.0
    for h in range(0, heads, 2):
        at = pl.ds(h * HD, 2 * HD)
        q2 = jnp.concatenate([q_ref[0, :, pl.ds(i * HD, HD)] for i in (h, h + 1)], axis=0)
        g2 = jnp.concatenate([g_ref[0, :, pl.ds(i * HD, HD)] for i in (h, h + 1)], axis=0)
        key_sum = key_sum + dot_nn(ds_ref[:, at], q2)
        value_sum = value_sum + dot_nn(p_ref[:, at], g2)
    for s, part in enumerate(part_refs):
        rows = slice(s * tokens, (s + 1) * tokens)
        part[:, :HD] = key_sum[rows].astype(BF16)
        part[:, HD:] = value_sum[rows].astype(BF16)


def query_kernel(n, heads, q_ref, g_ref, exp_ref, diff_ref, fac_ref, ds_ref, kv_ref, *refs):
    kv_refs, (dq_ref, own_ref) = refs[: n - 1], refs[n - 1 :]
    tokens = q_ref.shape[1]
    key_t = jnp.concatenate([kv_ref[:, :HD]] + [r[:, :HD] for r in kv_refs], axis=0).T
    key_sum, value_sum = 0.0, 0.0
    for h in range(heads):
        at = pl.ds(h * HD, HD)
        p = exp_ref[:, at] * fac_ref[h : h + 1, :]
        ds = (p * diff_ref[:, at]).astype(BF16)
        key_sum = key_sum + dot_nn(ds, q_ref[0, :, at])
        value_sum = value_sum + dot_nn(p.astype(BF16), g_ref[0, :, at])
        ds_all = jnp.concatenate([ds, ds_ref[:, at]], axis=0)
        dq_ref[0, :, at] = dot_nn(key_t, ds_all).T.astype(BF16)
    own_ref[:, :HD] = key_sum
    own_ref[:, HD:] = value_sum


def sum_kernel(own_ref, *refs):
    parts, (dk_ref, dv_ref) = refs[:-2], refs[-2:]
    total = own_ref[...]
    for part in parts:
        total = total + part[...].astype(F32)
    dk_ref[0] = total[:, :HD].astype(BF16)
    dv_ref[0] = total[:, HD:].astype(BF16)


def body(n, queries, keys, values, outputs, out_grad, positions, tile_flags):
    tokens, width = queries.shape[1:]
    heads = width // HD
    rank = lax.axis_index("row").astype(jnp.int32).reshape(1)
    pos = positions.reshape(n, tokens)
    sds = jax.ShapeDtypeStruct
    rows = (n - 1) * tokens

    def there(step):
        return [(i, peer_of(i, step, n)) for i in range(n)]

    def back(step):
        return [(j, i) for i, j in there(step)]

    keys, values, far_q, far_g, far_o = (
        pltpu.with_memory_space_constraint(x, pltpu.HBM) for x in (keys, values, queries, out_grad, outputs)
    )
    kv = pl.pallas_call(
        pack_kernel,
        out_shape=sds((tokens, 2 * HD), BF16),
        in_specs=[HBM] * 2,
        out_specs=VMEM,
        compiler_params=GRANT,
        scratch_shapes=[pltpu.SemaphoreType.DMA((2,))],
    )(keys, values)
    kv_far = [lax.ppermute(kv, "row", back(s)) for s in range(1, n)]
    bias, out_dot, top, total, e_own, diff, q_near, g_near = pl.pallas_call(
        functools.partial(pre_kernel, n, heads),
        out_shape=(
            sds((n, tokens, tokens), F32),
            sds((heads, tokens), F32),
            sds((heads, tokens), F32),
            sds((heads, tokens), F32),
            sds((tokens, width), F32),
            sds((tokens, width), F32),
            sds((1, tokens, width), BF16),
            sds((1, tokens, width), BF16),
        ),
        in_specs=[SMEM, SMEM, VMEM, HBM, HBM, HBM, VMEM],
        out_specs=(VMEM,) * 8,
        scratch_shapes=[pltpu.VMEM((1, tokens, width), BF16), pltpu.SemaphoreType.DMA((3,))],
        compiler_params=GRANT,
    )(rank, tile_flags, pos, far_q, far_g, far_o, kv)
    outs = pl.pallas_call(
        functools.partial(main_kernel, n, heads),
        out_shape=(sds((tokens, 2 * HD), BF16),) * (n - 1)
        + (sds((heads, tokens), F32), sds((rows, width), BF16)),
        in_specs=[VMEM] * (6 + n - 1),
        out_specs=(VMEM,) * (n + 1),
        compiler_params=GRANT,
        scratch_shapes=[pltpu.VMEM((rows, width), BF16)],
    )(q_near, g_near, bias, out_dot, top, total, *kv_far)
    parts, fac, ds = outs[: n - 1], outs[n - 1], outs[n]
    parts_in = [lax.ppermute(part, "row", there(s)) for s, part in list(zip(range(1, n), parts))[::-1]]
    query_grad, own = pl.pallas_call(
        functools.partial(query_kernel, n, heads),
        out_shape=(sds((1, tokens, width), BF16), sds((tokens, 2 * HD), F32)),
        in_specs=[VMEM] * (7 + n - 1),
        out_specs=(VMEM,) * 2,
        compiler_params=GRANT,
    )(q_near, g_near, e_own, diff, fac, ds, kv, *kv_far)
    key_grad, value_grad = pl.pallas_call(
        sum_kernel,
        out_shape=(sds((1, tokens, HD), BF16),) * 2,
        in_specs=[VMEM] * n,
        out_specs=(VMEM,) * 2,
        compiler_params=GRANT,
    )(own, *parts_in)
    return query_grad, key_grad, value_grad


def solution(mesh):
    whole = P("col", "row", None)
    return jax.shard_map(
        functools.partial(body, mesh.shape["row"]),
        mesh=mesh,
        in_specs=(whole,) * 5 + (P("col", None), whole),
        out_specs=(whole,) * 3,
        check_vma=False,
    )
```

time: 77.1 us -> 19.4 us (0.25)
  waiting for transfers between devices: 24.4 us -> 2.73 us
  blocking collectives: 18.5 us -> 0 us
  between operations: 14.2 us -> 0.67 us
  local copies, waits for them, and re-layouts: 10.4 us -> 0.68 us
  starting transfers between devices: 0.04 us -> 8.18 us
  Pallas kernels: 0 us -> 6.89 us
  matrix products: 4.77 us -> 0 us
  other arithmetic: 4.11 us -> 0 us
    reduce_scatter x1 -> x0, waiting for transfers between devices: 24.3 us -> none  [body(): lax.psum_scatter(jnp.concatenate([key_part, value_part], axis=1), 'row',...]
    all_gather x2 -> x0, blocking collectives: 18.5 us -> none  [the longest x1 10.1 us: body(): lax.all_gather(keys, 'row', axis=1, tiled=True)]
    ppermute x0 -> x6, starting transfers between devices: none -> 8.18 us  [the longest x3 4.63 us: body(): kv_far = [lax.ppermute(kv, 'row', back(s)) for s in range(1, n)]]
    pallas_call x0 -> x5, Pallas kernels: none -> 6.89 us  [the longest x1 2.21 us: body(): pl.pallas_call(functools.partial(pre_kernel, n, heads), out_shape=(sds((n...]
    unnamed x22 -> x4, local copies, waits for them, and re-layouts: 6.9 us -> 0.68 us
    dot_general x15 -> x0, matrix products: 4.77 us -> none  [the longest x8 2.35 us: block_scores(): jnp.einsum('qhd,kd->hqk', query_heads, key_piece, preferred_element_type=...]
    ppermute x0 -> x6, waiting for transfers between devices: none -> 2.73 us  [the longest x3 1.51 us: body(): lax.ppermute(part, 'row', there(s))]
    while x8 -> x0, local copies, waits for them, and re-layouts: 2.6 us -> none
  transfers between devices with their start and end apart: 1 -> 6, of which waited for: 1 -> 5; matrix products, arithmetic and copies ran while one was open for 2% -> 0% of each run, Pallas kernels for 0% -> 19%
where the time goes in v1:
time: 19.4 us; the launch traced here: 19.2 us
  starting transfers between devices  8.18 us (42%)
  Pallas kernels  6.89 us (36%)
  waiting for transfers between devices  2.73 us (14%)
  local copies, waits for them, and re-layouts  0.68 us (4%)
  between operations  0.67 us (3%)
    ppermute x3, starting transfers between devices, body(): kv_far = [lax.ppermute(kv, 'row', back(s)) for s in range(1, n)]  4.63 us
    ppermute x3, starting transfers between devices, body(): lax.ppermute(part, 'row', there(s))  3.55 us
    pallas_call x1, Pallas kernels, body(): pl.pallas_call(functools.partial(pre_kernel, n, heads), out_shape=(sds((n...  2.21 us
    pallas_call x1, Pallas kernels, body(): pl.pallas_call(functools.partial(main_kernel, n, heads), out_shape=(sds((...  1.82 us
    ppermute x3, waiting for transfers between devices, body(): lax.ppermute(part, 'row', there(s))  1.51 us
    pallas_call x1, Pallas kernels, body(): pl.pallas_call(functools.partial(query_kernel, n, heads), out_shape=(sds(...  1.42 us
    ppermute x3, waiting for transfers between devices, body(): kv_far = [lax.ppermute(kv, 'row', back(s)) for s in range(1, n)]  1.22 us
    pallas_call x1, Pallas kernels, body(): pl.pallas_call(pack_kernel, out_shape=sds((tokens, 2 * HD), BF16), in_spe...  0.79 us
  transfers between devices with their start and end apart: 6, of which 5 were waited for; matrix products, arithmetic and copies ran while one was open for 0% of the time, Pallas kernels for 19%

profile of v1, /device:TPU:0, one launch (start us, length us, event | category | flops | bytes accessed | tf_op | source)
XLA Modules:
  0.0 19.2 jit_solution(14520458737894668218)
XLA Ops:
  0.6 0.8 %shard_map.94.kv_ref = bf16[128,256]{1,0:T(8,128)(2,1)S(1)} custom-call(bf16[1,128,128]{2,1,0:T(8,128)(2,1)} %k_ref.1, bf16[1,128,128]{2,1,0:T(8,128)(2,1)} %v_ref.1), custom_call_target="tpu_custom_call" | custom-call | tf_op jit(solution)/shard_map/pallas_call | solution.py:168
  1.4 4.0 %collective-permute-start.2 = (bf16[128,256]{1,0:T(8,128)(2,1)S(1)}, bf16[128,256]{1,0:T(8,128)(2,1)S(1)}, u32[]{:S(2)}, u32[]{:S(2)}) collective-permute-start(bf16[128,256]{1,0:T(8,128)(2,1)S(1)} %shard_map.94.kv_ref), channel_id=1, source_target_pairs={{24,0},{16,8},{8,16},{0,24},{25,1},{17,9},{9,17},{1,25},{26,2},{18... | collective-permute-start | bytes 196616 | tf_op jit(solution)/shard_map/ppermute | solution.py:176
  5.4 0.5 %collective-permute-start.1 = (bf16[128,256]{1,0:T(8,128)(2,1)S(1)}, bf16[128,256]{1,0:T(8,128)(2,1)S(1)}, u32[]{:S(2)}, u32[]{:S(2)}) collective-permute-start(bf16[128,256]{1,0:T(8,128)(2,1)S(1)} %shard_map.94.kv_ref), channel_id=1, source_target_pairs={{16,0},{24,8},{0,16},{8,24},{17,1},{25,9},{1,17},{9,25},{18,2},{26... | collective-permute-start | bytes 196616 | tf_op jit(solution)/shard_map/ppermute | solution.py:176
  5.9 0.1 collective-permute-start
  6.1 0.0 copy-start
  6.1 0.0 copy-start.1
  6.1 0.7 %copy-done = s32[1,512]{1,0:T(1,128)S(1)} copy-done((s32[1,512]{1,0:T(1,128)S(1)}, s32[1,512]{1,0:T(1,128)}, u32[]{:S(2)}) %copy-start) | copy-done | bytes 2072
  6.7 0.0 copy-done.1
  6.7 2.2 %shard_map.95 = (f32[4,128,128]{2,1,0:T(8,128)S(1)}, f32[8,128]{1,0:T(8,128)S(1)}, f32[8,128]{1,0:T(8,128)S(1)}, f32[8,128]{1,0:T(8,128)S(1)}, f32[128,1024]{1,0...) custom-call(s32[1]{0:T(128)} %bitcast.rank_ref, ...), custom_call_target="tpu_custom_call" | custom-call | tf_op jit(solution)/shard_map/pallas_call | solution.py:177
  9.0 0.0 collective-permute-done.2.refs_2_
  9.0 0.7 %collective-permute-done.1.refs_1_ = bf16[128,256]{1,0:T(8,128)(2,1)S(1)} collective-permute-done((bf16[128,256]{1,0:T(8,128)(2,1)S(1)}, bf16[128,256]{1,0:T(8,128)(2,1)S(1)}, u32[]{:S(2)}, u32[]{:S(2)}) %collective-permute-start.1) | collective-permute-done | bytes 65568 | tf_op jit(solution)/shard_map/ppermute | solution.py:176
  9.7 0.5 %collective-permute-done.refs_0_ = bf16[128,256]{1,0:T(8,128)(2,1)S(1)} collective-permute-done((bf16[128,256]{1,0:T(8,128)(2,1)S(1)}, bf16[128,256]{1,0:T(8,128)(2,1)S(1)}, u32[]{:S(2)}, u32[]{:S(2)}) %collective-permute-start) | collective-permute-done | bytes 65568 | tf_op jit(solution)/shard_map/ppermute | solution.py:176
  10.2 1.8 %shard_map.96 = (bf16[128,256]{1,0:T(8,128)(2,1)S(1)}, bf16[128,256]{1,0:T(8,128)(2,1)S(1)}, bf16[128,256]{1,0:T(8,128)(2,1)S(1)}, f32[8,128]{1,0:T(8,128)S(1)}, bf16[384,1024]{1,0:T(8,128)(2,1)S(1)}) custom-call(bf16[1,128,1024]{2,1,0:T(8,128)(2,1)S(1)} %get-tuple-element.20.q_ref, bf16[1,128,1024]{2,1,0:T(8,128)(2,1)S(1)} %get-tuple-element.21.g_ref, ...), custom_call_target="tpu_custom_call" | custom-call | tf_op jit(solution)/shard_map/pallas_call | solution.py:194
  12.0 1.7 %collective-permute-start.3 = (bf16[128,256]{1,0:T(8,128)(2,1)S(1)}, bf16[128,256]{1,0:T(8,128)(2,1)S(1)}, u32[]{:S(2)}, u32[]{:S(2)}) collective-permute-start(bf16[128,256]{1,0:T(8,128)(2,1)S(1)} %get-tuple-element.32), channel_id=1, source_target_pairs={{0,24},{8,16},{16,8},{24,0},{1,25},{9,17},{17,9},{25,1},{2,26},{10... | collective-permute-start | bytes 196616 | tf_op jit(solution)/shard_map/ppermute | solution.py:204
  13.7 0.5 %collective-permute-start.4 = (bf16[128,256]{1,0:T(8,128)(2,1)S(1)}, bf16[128,256]{1,0:T(8,128)(2,1)S(1)}, u32[]{:S(2)}, u32[]{:S(2)}) collective-permute-start(bf16[128,256]{1,0:T(8,128)(2,1)S(1)} %get-tuple-element.33), channel_id=1, source_target_pairs={{0,16},{8,24},{16,0},{24,8},{1,17},{9,25},{17,1},{25,9},{2,18},{10... | collective-permute-start | bytes 196616 | tf_op jit(solution)/shard_map/ppermute | solution.py:204
  14.2 1.3 %collective-permute-start.5 = (bf16[128,256]{1,0:T(8,128)(2,1)S(1)}, bf16[128,256]{1,0:T(8,128)(2,1)S(1)}, u32[]{:S(2)}, u32[]{:S(2)}) collective-permute-start(bf16[128,256]{1,0:T(8,128)(2,1)S(1)} %get-tuple-element.34), channel_id=1, source_target_pairs={{0,8},{8,0},{16,24},{24,16},{1,9},{9,1},{17,25},{25,17},{2,10},{10... | collective-permute-start | bytes 196616 | tf_op jit(solution)/shard_map/ppermute | solution.py:204
  15.6 1.4 %shard_map.97 = (bf16[1,128,1024]{2,1,0:T(8,128)(2,1)}, f32[128,256]{1,0:T(8,128)S(1)}) custom-call(bf16[1,128,1024]{2,1,0:T(8,128)(2,1)S(1)} %get-tuple-element.20.q_ref, bf16[1,128,1024]{2,1,0:T(8,128)(2,1)S(1)} %get-tuple-element.21.g_ref, f32[128,1024]{1,0:T(8,128)S(1)} %get-tuple-element.22.exp_ref, f32[128,1024]{1,0:T(8,128)S(1)} %get-tuple-element.23.diff_ref, ...), custom_call_target="tpu_custom_call" | custom-call | tf_op jit(solution)/shard_map/pallas_call | solution.py:205
  17.0 0.7 %collective-permute-done.3.refs_0_ = bf16[128,256]{1,0:T(8,128)(2,1)S(1)} collective-permute-done((bf16[128,256]{1,0:T(8,128)(2,1)S(1)}, bf16[128,256]{1,0:T(8,128)(2,1)S(1)}, u32[]{:S(2)}, u32[]{:S(2)}) %collective-permute-start.3) | collective-permute-done | bytes 65568 | tf_op jit(solution)/shard_map/ppermute | solution.py:204
  17.7 0.6 %collective-permute-done.4.refs_1_ = bf16[128,256]{1,0:T(8,128)(2,1)S(1)} collective-permute-done((bf16[128,256]{1,0:T(8,128)(2,1)S(1)}, bf16[128,256]{1,0:T(8,128)(2,1)S(1)}, u32[]{:S(2)}, u32[]{:S(2)}) %collective-permute-start.4) | collective-permute-done | bytes 65568 | tf_op jit(solution)/shard_map/ppermute | solution.py:204
  18.3 0.2 collective-permute-done.5.refs_2_
  18.5 0.7 %shard_map.98 = (bf16[1,128,128]{2,1,0:T(8,128)(2,1)}, bf16[1,128,128]{2,1,0:T(8,128)(2,1)}) custom-call(f32[128,256]{1,0:T(8,128)S(1)} %get-tuple-element.31.own_ref, bf16[128,256]{1,0:T(8,128)(2,1)S(1)} %collective-permute-done.3.refs_0_, bf16[128,256]{1,0:T(8,128)(2,1)S(1)} %collective-permute-done.4.refs_1_, ...), custom_call_target="tpu_custom_call" | custom-call | tf_op jit(solution)/shard_map/pallas_call | solution.py:212
Async XLA Ops:
  1.4 7.5 %collective-permute-start.2 = (bf16[128,256]{1,0:T(8,128)(2,1)S(1)}, bf16[128,256]{1,0:T(8,128)(2,1)S(1)}, u32[]{:S(2)}, u32[]{:S(2)}) collective-permute-start(bf16[128,256]{1,0:T(8,128)(2,1)S(1)} %shard_map.94.kv_ref), channel_id=1, source_target_pairs={{24,0},{16,8},{8,16},{0,24},{25,1},{17,9},{9,17},{1,25},{26,2},{18... | collective-permute-start | bytes 196616 | tf_op jit(solution)/shard_map/ppermute | solution.py:176
  5.4 4.3 %collective-permute-start.1 = (bf16[128,256]{1,0:T(8,128)(2,1)S(1)}, bf16[128,256]{1,0:T(8,128)(2,1)S(1)}, u32[]{:S(2)}, u32[]{:S(2)}) collective-permute-start(bf16[128,256]{1,0:T(8,128)(2,1)S(1)} %shard_map.94.kv_ref), channel_id=1, source_target_pairs={{16,0},{24,8},{0,16},{8,24},{17,1},{25,9},{1,17},{9,25},{18,2},{26... | collective-permute-start | bytes 196616 | tf_op jit(solution)/shard_map/ppermute | solution.py:176
  5.9 4.3 %collective-permute-start = (bf16[128,256]{1,0:T(8,128)(2,1)S(1)}, bf16[128,256]{1,0:T(8,128)(2,1)S(1)}, u32[]{:S(2)}, u32[]{:S(2)}) collective-permute-start(bf16[128,256]{1,0:T(8,128)(2,1)S(1)} %shard_map.94.kv_ref), channel_id=1, source_target_pairs={{8,0},{0,8},{24,16},{16,24},{9,1},{1,9},{25,17},{17,25},{10,2},{2,... | collective-permute-start | bytes 196616 | tf_op jit(solution)/shard_map/ppermute | solution.py:176
  6.1 0.7 %copy-start = (s32[1,512]{1,0:T(1,128)S(1)}, s32[1,512]{1,0:T(1,128)}, u32[]{:S(2)}) copy-start(s32[1,512]{1,0:T(1,128)} %param.12) | copy-start | bytes 6148
  6.1 0.7 %copy-start.1 = (s32[1,1,4]{2,1,0:T(1,128)S(1)}, s32[1,1,4]{2,1,0:T(1,128)}, u32[]{:S(2)}) copy-start(s32[1,1,4]{2,1,0:T(1,128)} %flag_ref.1) | copy-start | bytes 52
  12.0 5.7 %collective-permute-start.3 = (bf16[128,256]{1,0:T(8,128)(2,1)S(1)}, bf16[128,256]{1,0:T(8,128)(2,1)S(1)}, u32[]{:S(2)}, u32[]{:S(2)}) collective-permute-start(bf16[128,256]{1,0:T(8,128)(2,1)S(1)} %get-tuple-element.32), channel_id=1, source_target_pairs={{0,24},{8,16},{16,8},{24,0},{1,25},{9,17},{17,9},{25,1},{2,26},{10... | collective-permute-start | bytes 196616 | tf_op jit(solution)/shard_map/ppermute | solution.py:204
  13.7 4.6 %collective-permute-start.4 = (bf16[128,256]{1,0:T(8,128)(2,1)S(1)}, bf16[128,256]{1,0:T(8,128)(2,1)S(1)}, u32[]{:S(2)}, u32[]{:S(2)}) collective-permute-start(bf16[128,256]{1,0:T(8,128)(2,1)S(1)} %get-tuple-element.33), channel_id=1, source_target_pairs={{0,16},{8,24},{16,0},{24,8},{1,17},{9,25},{17,1},{25,9},{2,18},{10... | collective-permute-start | bytes 196616 | tf_op jit(solution)/shard_map/ppermute | solution.py:204
  14.2 4.3 %collective-permute-start.5 = (bf16[128,256]{1,0:T(8,128)(2,1)S(1)}, bf16[128,256]{1,0:T(8,128)(2,1)S(1)}, u32[]{:S(2)}, u32[]{:S(2)}) collective-permute-start(bf16[128,256]{1,0:T(8,128)(2,1)S(1)} %get-tuple-element.34), channel_id=1, source_target_pairs={{0,8},{8,0},{16,24},{24,16},{1,9},{9,1},{17,25},{25,17},{2,10},{10... | collective-permute-start | bytes 196616 | tf_op jit(solution)/shard_map/ppermute | solution.py:204
